TPU v7x, 256 devices: a whole 4x4x8 slice. The times are simulated.
256 devices in a mesh: row: 16 (over z, core), col: 16 (over x, y).
Axes of the slice: x: 4, y: 4, z: 8, core: 2. Of those that a mesh axis runs over, the one named last changes fastest.
Arguments:
- gen_showers: bfloat16 [16384, 6480], P(('row', 'col')), may hold values from -10 to 10
- ref_showers: bfloat16 [16384, 6480], P(('row', 'col')), may hold values from -10 to 10
- w_in: bfloat16 [6480, 512], replicated, may hold values from -0.078125 to 0.078125
- b_in: float32 [512], replicated, may hold values from -4 to 4
- w_out: bfloat16 [512, 256], replicated, may hold values from -0.25 to 0.25
Outputs:
- gen_potential: float32 [16384], P('row')
- ref_potential: float32 [16, 1024], P(None, 'col')
All inputs are finite; a program needn't handle non-finite values.
Results may differ from a plain program's by a relative error of at most 0.0003.
Values sent between devices are 32-bit elements; how exact they have to be, the bound alone decides.
A program may use at most 128 MiB of HBM per device.

v0:
```python
import math
import jax
import jax.numpy as jnp
from jax import lax
from jax.sharding import PartitionSpec as P

ITERS = 3
EPSILON = 0.1


def embed(showers, w_in, b_in, w_out):
    hidden = jnp.dot(showers, w_in, preferred_element_type=jnp.float32) + b_in
    hidden = jnp.maximum(hidden, 0.0)
    features = jnp.dot(hidden, w_out.astype(jnp.float32), precision=lax.Precision.HIGHEST)
    squares = jnp.sum(jnp.square(features), axis=1)
    return (features, squares)


def reduce_cols(scaled):
    largest = lax.pmax(jnp.max(scaled, axis=1), "col")
    totals = lax.psum(jnp.sum(jnp.exp(scaled - largest[:, None]), axis=1), "col")
    return -EPSILON * (largest + jnp.log(totals))


def reduce_rows(scaled):
    largest = lax.pmax(jnp.max(scaled, axis=0), "row")
    totals = lax.psum(jnp.sum(jnp.exp(scaled - largest[None, :]), axis=0), "row")
    return -EPSILON * (largest + jnp.log(totals))


def body(gen_showers, ref_showers, w_in, b_in, w_out):
    gen_feat, gen_sq = embed(gen_showers, w_in, b_in, w_out)
    ref_feat, ref_sq = embed(ref_showers, w_in, b_in, w_out)
    row_count = lax.axis_size("row")
    col_count = lax.axis_size("col")
    per_dev = gen_feat.shape[0]
    width = gen_feat.shape[1]
    gen_rows, gen_norms = (
        lax.all_gather(gen_feat, "col", axis=0, tiled=True),
        lax.all_gather(gen_sq, "col", axis=0, tiled=True),
    )
    ref_cols, ref_norms = (
        lax.all_gather(ref_feat, "row", axis=0, tiled=True),
        lax.all_gather(ref_sq, "row", axis=0, tiled=True),
    )
    total_count = row_count * col_count * per_dev
    log_weight = -math.log(total_count)

    def tile_cost():
        inner_prod = lax.dot_general(
            gen_rows,
            ref_cols,
            (((1,), (1,)), ((), ())),
            precision=lax.Precision.HIGHEST,
            preferred_element_type=jnp.float32,
        )
        return (gen_norms[:, None] + ref_norms[None, :] - 2.0 * inner_prod) / width

    ref_pot = jnp.zeros((ref_cols.shape[0],), jnp.float32)
    gen_pot = jnp.zeros((gen_rows.shape[0],), jnp.float32)
    for sweep_idx in range(ITERS):
        scaled = log_weight + (ref_pot[None, :] - tile_cost()) / EPSILON
        gen_pot = reduce_cols(scaled)
        scaled = log_weight + (gen_pot[:, None] - tile_cost()) / EPSILON
        ref_pot = reduce_rows(scaled)
    return (gen_pot, ref_pot.reshape(row_count, per_dev))


def solution(mesh):
    return jax.shard_map(
        body,
        mesh=mesh,
        in_specs=(P(("row", "col"), None), P(("row", "col"), None), P(), P(), P()),
        out_specs=(P("row"), P(None, "col")),
        check_vma=False,
    )
```

profile of v0, /device:TPU:1, one launch (start us, length us, event | category | flops | bytes accessed | tf_op | source)
XLA Modules:
  0.0 517.0 jit_solution(4666240185190480455)
XLA Ops:
  7.3 1.1 copy-done
  8.4 4.1 fusion.7
  12.6 1.0 multiply_reduce_fusion.1
  13.7 4.1 fusion.6
  17.8 1.0 multiply_reduce_fusion
  21.8 34.3 %all-reduce = f32[1024]{0:T(1024)S(1)} all-reduce(f32[1024]{0:T(1024)S(1)} %dynamic-update-slice), channel_id=1, replica_groups=mesh['row'=16,'col'=16] {'col'}, use_global_device_ids=true, to_apply=%add | all-reduce | flops 1024 | bytes 8192
  56.1 34.0 %all-reduce.1 = f32[1024]{0:T(1024)S(1)} all-reduce(f32[1024]{0:T(1024)S(1)} %dynamic-update-slice.1), channel_id=1, replica_groups=mesh['row'=16,'col'=16] {'row'}, use_global_device_ids=true, to_apply=%add.1 | all-reduce | flops 1024 | bytes 8192
  90.2 14.9 %all-gather.5.cloned.1.call-done = f32[1024,256]{1,0:T(8,128)} async-done(((f32[64,256]{1,0:T(8,128)}), f32[1024,256]{1,0:T(8,128)}) %all-gather.5.cloned.1.call-update) | async-done | bytes 1048592 | tf_op jit(solution)/shard_map/all_gather | solution.py:43
  105.1 7.9 %fusion = (f32[1024]{0:T(1024)S(1)}, f32[1024,1024]{1,0:T(8,128)}) fusion(f32[1024,256]{1,0:T(8,128)} %all-gather.3.cloned.1.call-done, f32[1024,256]{1,0:T(8,128)} %all-gather.5.cloned.1.call-done, f32[1024]{0:T(1024)S(1)} %all-reduce.1, f32[1024]{0:T(1024)S(1)} %all-reduce), kind=kOutput, calls=%fused_computation.13 | convolution fusion | flops 3229613056 | bytes 6303744 | tf_op jit(solution)/shard_map/dot_general | solution.py:50
  113.0 33.2 %pmax.42 = f32[1024]{0:T(1024)S(1)} all-reduce(f32[1024]{0:T(1024)S(1)} %get-tuple-element.6), channel_id=1, replica_groups=mesh['row'=16,'col'=16] {'col'}, use_global_device_ids=true, to_apply=%region_3.0 | all-reduce | flops 1024 | bytes 8192 | tf_op jit(solution)/shard_map/pmax | solution.py:20
  146.2 3.3 exponential_reduce_fusion.5
  149.5 28.5 %psum.42 = f32[1024]{0:T(1024)S(1)} all-reduce(f32[1024]{0:T(1024)S(1)} %exponential_reduce_fusion.5), channel_id=1, replica_groups=mesh['row'=16,'col'=16] {'col'}, use_global_device_ids=true, to_apply=%region_5.0 | all-reduce | flops 1024 | bytes 8192 | tf_op jit(solution)/shard_map/psum | solution.py:21
  178.0 2.8 fusion.1
  180.8 37.2 %pmax.43 = f32[1024]{0:T(1024)S(1)} all-reduce(f32[1024]{0:T(1024)S(1)} %fusion.1), channel_id=1, replica_groups=mesh['row'=16,'col'=16] {'row'}, use_global_device_ids=true, to_apply=%region_7.0 | all-reduce | flops 1024 | bytes 8192 | tf_op jit(solution)/shard_map/pmax | solution.py:26
  218.1 3.2 exponential_reduce_fusion.4
  221.3 23.6 %psum.43 = f32[1024]{0:T(1024)S(1)} all-reduce(f32[1024]{0:T(1024)S(1)} %exponential_reduce_fusion.4), channel_id=1, replica_groups=mesh['row'=16,'col'=16] {'row'}, use_global_device_ids=true, to_apply=%region_9.0 | all-reduce | flops 1024 | bytes 8192 | tf_op jit(solution)/shard_map/psum | solution.py:27
  244.8 2.8 fusion.2
  247.7 30.4 %pmax.44 = f32[1024]{0:T(1024)S(1)} all-reduce(f32[1024]{0:T(1024)S(1)} %fusion.2), channel_id=1, replica_groups=mesh['row'=16,'col'=16] {'col'}, use_global_device_ids=true, to_apply=%region_11.0 | all-reduce | flops 1024 | bytes 8192 | tf_op jit(solution)/shard_map/pmax | solution.py:20
  278.1 3.3 exponential_reduce_fusion.3
  281.4 28.5 %psum.44 = f32[1024]{0:T(1024)S(1)} all-reduce(f32[1024]{0:T(1024)S(1)} %exponential_reduce_fusion.3), channel_id=1, replica_groups=mesh['row'=16,'col'=16] {'col'}, use_global_device_ids=true, to_apply=%region_13.0 | all-reduce | flops 1024 | bytes 8192 | tf_op jit(solution)/shard_map/psum | solution.py:21
  309.9 2.8 fusion.3
  312.7 37.7 %pmax.45 = f32[1024]{0:T(1024)S(1)} all-reduce(f32[1024]{0:T(1024)S(1)} %fusion.3), channel_id=1, replica_groups=mesh['row'=16,'col'=16] {'row'}, use_global_device_ids=true, to_apply=%region_15.0 | all-reduce | flops 1024 | bytes 8192 | tf_op jit(solution)/shard_map/pmax | solution.py:26
  350.4 3.2 exponential_reduce_fusion.2
  353.7 23.6 %psum.45 = f32[1024]{0:T(1024)S(1)} all-reduce(f32[1024]{0:T(1024)S(1)} %exponential_reduce_fusion.2), channel_id=1, replica_groups=mesh['row'=16,'col'=16] {'row'}, use_global_device_ids=true, to_apply=%region_17.0 | all-reduce | flops 1024 | bytes 8192 | tf_op jit(solution)/shard_map/psum | solution.py:27
  377.2 2.8 fusion.4
  380.0 30.2 %pmax.46 = f32[1024]{0:T(1024)S(1)} all-reduce(f32[1024]{0:T(1024)S(1)} %fusion.4), channel_id=1, replica_groups=mesh['row'=16,'col'=16] {'col'}, use_global_device_ids=true, to_apply=%region_19.0 | all-reduce | flops 1024 | bytes 8192 | tf_op jit(solution)/shard_map/pmax | solution.py:20
  410.3 3.3 exponential_reduce_fusion.1
  413.6 28.5 %psum.46 = f32[1024]{0:T(1024)S(1)} all-reduce(f32[1024]{0:T(1024)S(1)} %exponential_reduce_fusion.1), channel_id=1, replica_groups=mesh['row'=16,'col'=16] {'col'}, use_global_device_ids=true, to_apply=%region_21.0 | all-reduce | flops 1024 | bytes 8192 | tf_op jit(solution)/shard_map/psum | solution.py:21
  442.1 2.8 fusion.5
  444.9 37.8 %pmax.47 = f32[1024]{0:T(1024)S(1)} all-reduce(f32[1024]{0:T(1024)S(1)} %fusion.5), channel_id=1, replica_groups=mesh['row'=16,'col'=16] {'row'}, use_global_device_ids=true, to_apply=%region_23.0 | all-reduce | flops 1024 | bytes 8192 | tf_op jit(solution)/shard_map/pmax | solution.py:26
  482.7 3.2 exponential_reduce_fusion
  485.9 23.6 %psum.47 = f32[1024]{0:T(1024)S(1)} all-reduce(f32[1024]{0:T(1024)S(1)} %exponential_reduce_fusion), channel_id=1, replica_groups=mesh['row'=16,'col'=16] {'row'}, use_global_device_ids=true, to_apply=%region_25.0 | all-reduce | flops 1024 | bytes 8192 | tf_op jit(solution)/shard_map/psum | solution.py:27
  (31 shorter events, 2.5 us)
Async XLA Ops:
  7.2 1.2 copy-start
  7.2 6.5 %copy-start.4 = (f32[512]{0:T(512)S(1)}, f32[512]{0:T(512)}, u32[]{:S(2)}) copy-start(f32[512]{0:T(512)} %param.8) | copy-start | bytes 6148
  7.2 5.4 %copy-start.2 = (bf16[512,256]{1,0:T(8,128)(2,1)S(1)}, bf16[512,256]{1,0:T(8,128)(2,1)}, u32[]{:S(2)}) copy-start(bf16[512,256]{1,0:T(8,128)(2,1)} %param.9) | copy-start | bytes 786436
  7.2 6.5 %copy-start.1 = (bf16[64,6480]{1,0:T(8,128)(2,1)S(1)}, bf16[64,6480]{1,0:T(8,128)(2,1)}, u32[]{:S(2)}) copy-start(bf16[64,6480]{1,0:T(8,128)(2,1)} %param.6) | copy-start | bytes 2488324
  7.2 82.9 %all-gather.3.cloned.1.call-start = ((), (), s32[]{:S(2)}) async-start(), calls=%async_computation | async-start | bytes 1114112 | tf_op jit(solution)/shard_map/all_gather | solution.py:39
  13.6 5.3 %copy-start.6 = (u32[256]{0:T(256)S(1)}, u32[256]{0:T(256)}, u32[]{:S(2)}) copy-start(u32[256]{0:T(256)} %constant.32) | copy-start | bytes 3076
  13.6 5.9 %copy-start.5 = (u32[256]{0:T(256)S(1)}, u32[256]{0:T(256)}, u32[]{:S(2)}) copy-start(u32[256]{0:T(256)} %constant.27) | copy-start | bytes 3076
  13.6 91.5 %all-gather.5.cloned.1.call-start = ((), (), s32[]{:S(2)}) async-start(), calls=%async_computation.1 | async-start | bytes 1114112 | tf_op jit(solution)/shard_map/all_gather | solution.py:43
  442.1 43.8 %copy-start.3 = (f32[1024]{0:T(1024)}, f32[1024]{0:T(1024)S(1)}, u32[]{:S(2)}) copy-start(f32[1024]{0:T(1024)S(1)} %add_multiply_fusion.1) | copy-start | bytes 12292
Sparse Core Ops, SparseCore 0:
  13.7 49.8 all-gather.2
  65.4 39.5 all-gather.4
where the time goes:
time: 518 us; the launch traced here: 517 us
  blocking collectives  431 us (83%)
  other arithmetic  33.6 us (6%)
  matrix products  18.2 us (4%)
  between operations  15.5 us (3%)
  waiting for transfers between devices  15 us (3%)
    pmax x3, blocking collectives, reduce_rows(): largest = lax.pmax(jnp.max(scaled, axis=0), 'row')  113 us
    pmax x3, blocking collectives, reduce_cols(): largest = lax.pmax(jnp.max(scaled, axis=1), 'col')  93.9 us
    psum x3, blocking collectives, reduce_cols(): lax.psum(jnp.sum(jnp.exp(scaled - largest[:, None]), axis=1), 'col')  85.5 us
    psum x3, blocking collectives, reduce_rows(): lax.psum(jnp.sum(jnp.exp(scaled - largest[None, :]), axis=0), 'row')  70.7 us
    unnamed x2, blocking collectives  68.3 us
    all_gather x1, waiting for transfers between devices, body(): lax.all_gather(ref_feat, 'row', axis=0, tiled=True)  14.9 us
  transfers between devices with their start and end apart: 2, of which 1 were waited for; matrix products, arithmetic and copies ran while one was open for 1% of the time, Pallas kernels for 0%

commit v1 on v0

--- a/solution.py
+++ b/solution.py
@@ -24,7 +24,11 @@
 
 def reduce_rows(scaled):
     largest = lax.pmax(jnp.max(scaled, axis=0), "row")
-    totals = lax.psum(jnp.sum(jnp.exp(scaled - largest[None, :]), axis=0), "row")
+
+    def _perform_samples_all(inp):
+        return jnp.sum(lax.all_gather(inp, "row"), 0)
+
+    totals = _perform_samples_all(jnp.sum(jnp.exp(scaled - largest[None, :]), axis=0))
     return -EPSILON * (largest + jnp.log(totals))
 
 

time: 518 us -> 491 us (0.948)
  blocking collectives: 431 us -> 404 us
    psum x3 -> x0, blocking collectives: 70.7 us -> none  [reduce_rows(): lax.psum(jnp.sum(jnp.exp(scaled - largest[None, :]), axis=0), 'row')]
    all_gather x0 -> x3, blocking collectives: none -> 44.4 us  [_perform_samples_all(): return jnp.sum(lax.all_gather(inp, 'row'), 0)]
where the time goes in v1:
time: 491 us; the launch traced here: 490 us
  blocking collectives  404 us (82%)
  other arithmetic  33.6 us (7%)
  matrix products  18.2 us (4%)
  between operations  15.6 us (3%)
  waiting for transfers between devices  15 us (3%)
    pmax x3, blocking collectives, reduce_rows(): largest = lax.pmax(jnp.max(scaled, axis=0), 'row')  112 us
    pmax x3, blocking collectives, reduce_cols(): largest = lax.pmax(jnp.max(scaled, axis=1), 'col')  93.9 us
    psum x3, blocking collectives, reduce_cols(): lax.psum(jnp.sum(jnp.exp(scaled - largest[:, None]), axis=1), 'col')  85.6 us
    unnamed x2, blocking collectives  68.3 us
    all_gather x3, blocking collectives, _perform_samples_all(): return jnp.sum(lax.all_gather(inp, 'row'), 0)  44.4 us
    all_gather x1, waiting for transfers between devices, body(): lax.all_gather(ref_feat, 'row', axis=0, tiled=True)  14.9 us
    reduce_sum x3, other arithmetic, reduce_cols(): jnp.sum(jnp.exp(scaled - largest[:, None]), axis=1)  9.88 us
  transfers between devices with their start and end apart: 2, of which 1 were waited for; matrix products, arithmetic and copies ran while one was open for 1% of the time, Pallas kernels for 0%

profile of v1, /device:TPU:1, one launch (start us, length us, event | category | flops | bytes accessed | tf_op | source)
XLA Modules:
  0.0 489.9 jit_solution(3651629564114793598)
XLA Ops:
  7.3 1.1 copy-done
  8.4 4.1 fusion.7
  12.6 1.0 multiply_reduce_fusion.1
  13.7 4.1 fusion.6
  17.8 1.0 multiply_reduce_fusion
  21.8 34.3 %all-reduce = f32[1024]{0:T(1024)S(1)} all-reduce(f32[1024]{0:T(1024)S(1)} %dynamic-update-slice), channel_id=1, replica_groups=mesh['row'=16,'col'=16] {'col'}, use_global_device_ids=true, to_apply=%add | all-reduce | flops 1024 | bytes 8192
  56.1 34.0 %all-reduce.1 = f32[1024]{0:T(1024)S(1)} all-reduce(f32[1024]{0:T(1024)S(1)} %dynamic-update-slice.1), channel_id=1, replica_groups=mesh['row'=16,'col'=16] {'row'}, use_global_device_ids=true, to_apply=%add.1 | all-reduce | flops 1024 | bytes 8192
  90.2 14.9 %all-gather.8.cloned.1.call-done = f32[1024,256]{1,0:T(8,128)} async-done(((f32[64,256]{1,0:T(8,128)}), f32[1024,256]{1,0:T(8,128)}) %all-gather.8.cloned.1.call-update) | async-done | bytes 1048592 | tf_op jit(solution)/shard_map/all_gather | solution.py:47
  105.1 7.9 %fusion = (f32[1024]{0:T(1024)S(1)}, f32[1024,1024]{1,0:T(8,128)}) fusion(f32[1024,256]{1,0:T(8,128)} %all-gather.6.cloned.1.call-done, f32[1024,256]{1,0:T(8,128)} %all-gather.8.cloned.1.call-done, f32[1024]{0:T(1024)S(1)} %all-reduce.1, f32[1024]{0:T(1024)S(1)} %all-reduce), kind=kOutput, calls=%fused_computation.13 | convolution fusion | flops 3229613056 | bytes 6303744 | tf_op jit(solution)/shard_map/dot_general | solution.py:54
  113.0 33.2 %pmax.42 = f32[1024]{0:T(1024)S(1)} all-reduce(f32[1024]{0:T(1024)S(1)} %get-tuple-element.6), channel_id=1, replica_groups=mesh['row'=16,'col'=16] {'col'}, use_global_device_ids=true, to_apply=%region_3.0 | all-reduce | flops 1024 | bytes 8192 | tf_op jit(solution)/shard_map/pmax | solution.py:20
  146.2 3.3 exponential_reduce_fusion.5
  149.5 28.5 %psum.21 = f32[1024]{0:T(1024)S(1)} all-reduce(f32[1024]{0:T(1024)S(1)} %exponential_reduce_fusion.5), channel_id=1, replica_groups=mesh['row'=16,'col'=16] {'col'}, use_global_device_ids=true, to_apply=%region_5.0 | all-reduce | flops 1024 | bytes 8192 | tf_op jit(solution)/shard_map/psum | solution.py:21
  178.0 2.8 fusion.1
  180.8 37.2 %pmax.43 = f32[1024]{0:T(1024)S(1)} all-reduce(f32[1024]{0:T(1024)S(1)} %fusion.1), channel_id=1, replica_groups=mesh['row'=16,'col'=16] {'row'}, use_global_device_ids=true, to_apply=%region_7.0 | all-reduce | flops 1024 | bytes 8192 | tf_op jit(solution)/shard_map/pmax | solution.py:26
  218.1 3.2 exponential_reduce_fusion.4
  221.3 14.8 %all-gather = f32[16384]{0:T(1024)S(1)} all-gather(f32[1024]{0:T(1024)S(1)} %exponential_reduce_fusion.4), channel_id=2, replica_groups=mesh['row'=16,'col'=16] {'row'}, dimensions={0}, use_global_device_ids=true | all-gather | bytes 69632 | tf_op jit(solution)/shard_map/all_gather | solution.py:29
  236.2 2.8 fusion.2
  239.0 30.4 %pmax.44 = f32[1024]{0:T(1024)S(1)} all-reduce(f32[1024]{0:T(1024)S(1)} %fusion.2), channel_id=1, replica_groups=mesh['row'=16,'col'=16] {'col'}, use_global_device_ids=true, to_apply=%region_11.0 | all-reduce | flops 1024 | bytes 8192 | tf_op jit(solution)/shard_map/pmax | solution.py:20
  269.4 3.3 exponential_reduce_fusion.3
  272.7 28.5 %psum.22 = f32[1024]{0:T(1024)S(1)} all-reduce(f32[1024]{0:T(1024)S(1)} %exponential_reduce_fusion.3), channel_id=1, replica_groups=mesh['row'=16,'col'=16] {'col'}, use_global_device_ids=true, to_apply=%region_13.0 | all-reduce | flops 1024 | bytes 8192 | tf_op jit(solution)/shard_map/psum | solution.py:21
  301.2 2.8 fusion.3
  304.0 37.3 %pmax.45 = f32[1024]{0:T(1024)S(1)} all-reduce(f32[1024]{0:T(1024)S(1)} %fusion.3), channel_id=1, replica_groups=mesh['row'=16,'col'=16] {'row'}, use_global_device_ids=true, to_apply=%region_15.0 | all-reduce | flops 1024 | bytes 8192 | tf_op jit(solution)/shard_map/pmax | solution.py:26
  341.3 3.2 exponential_reduce_fusion.2
  344.5 14.8 %all-gather.1 = f32[16384]{0:T(1024)S(1)} all-gather(f32[1024]{0:T(1024)S(1)} %exponential_reduce_fusion.2), channel_id=3, replica_groups=mesh['row'=16,'col'=16] {'row'}, dimensions={0}, use_global_device_ids=true | all-gather | bytes 69632 | tf_op jit(solution)/shard_map/all_gather | solution.py:29
  359.4 2.8 fusion.4
  362.2 30.2 %pmax.46 = f32[1024]{0:T(1024)S(1)} all-reduce(f32[1024]{0:T(1024)S(1)} %fusion.4), channel_id=1, replica_groups=mesh['row'=16,'col'=16] {'col'}, use_global_device_ids=true, to_apply=%region_19.0 | all-reduce | flops 1024 | bytes 8192 | tf_op jit(solution)/shard_map/pmax | solution.py:20
  392.4 3.3 exponential_reduce_fusion.1
  395.7 28.5 %psum.23 = f32[1024]{0:T(1024)S(1)} all-reduce(f32[1024]{0:T(1024)S(1)} %exponential_reduce_fusion.1), channel_id=1, replica_groups=mesh['row'=16,'col'=16] {'col'}, use_global_device_ids=true, to_apply=%region_21.0 | all-reduce | flops 1024 | bytes 8192 | tf_op jit(solution)/shard_map/psum | solution.py:21
  424.2 2.8 fusion.5
  427.1 37.2 %pmax.47 = f32[1024]{0:T(1024)S(1)} all-reduce(f32[1024]{0:T(1024)S(1)} %fusion.5), channel_id=1, replica_groups=mesh['row'=16,'col'=16] {'row'}, use_global_device_ids=true, to_apply=%region_23.0 | all-reduce | flops 1024 | bytes 8192 | tf_op jit(solution)/shard_map/pmax | solution.py:26
  464.3 3.2 exponential_reduce_fusion
  467.5 14.8 %all-gather.2 = f32[16384]{0:T(1024)S(1)} all-gather(f32[1024]{0:T(1024)S(1)} %exponential_reduce_fusion), channel_id=4, replica_groups=mesh['row'=16,'col'=16] {'row'}, dimensions={0}, use_global_device_ids=true | all-gather | bytes 69632 | tf_op jit(solution)/shard_map/all_gather | solution.py:29
  (37 shorter events, 2.6 us)
Async XLA Ops:
  7.2 1.2 copy-start
  7.2 6.5 %copy-start.4 = (f32[512]{0:T(512)S(1)}, f32[512]{0:T(512)}, u32[]{:S(2)}) copy-start(f32[512]{0:T(512)} %param.8) | copy-start | bytes 6148
  7.2 5.4 %copy-start.2 = (bf16[512,256]{1,0:T(8,128)(2,1)S(1)}, bf16[512,256]{1,0:T(8,128)(2,1)}, u32[]{:S(2)}) copy-start(bf16[512,256]{1,0:T(8,128)(2,1)} %param.9) | copy-start | bytes 786436
  7.2 6.5 %copy-start.1 = (bf16[64,6480]{1,0:T(8,128)(2,1)S(1)}, bf16[64,6480]{1,0:T(8,128)(2,1)}, u32[]{:S(2)}) copy-start(bf16[64,6480]{1,0:T(8,128)(2,1)} %param.6) | copy-start | bytes 2488324
  7.2 82.9 %all-gather.6.cloned.1.call-start = ((), (), s32[]{:S(2)}) async-start(), calls=%async_computation | async-start | bytes 1114112 | tf_op jit(solution)/shard_map/all_gather | solution.py:43
  13.6 5.3 %copy-start.6 = (u32[256]{0:T(256)S(1)}, u32[256]{0:T(256)}, u32[]{:S(2)}) copy-start(u32[256]{0:T(256)} %constant.27) | copy-start | bytes 3076
  13.6 5.9 %copy-start.5 = (u32[256]{0:T(256)S(1)}, u32[256]{0:T(256)}, u32[]{:S(2)}) copy-start(u32[256]{0:T(256)} %constant.32) | copy-start | bytes 3076
  13.6 91.5 %all-gather.8.cloned.1.call-start = ((), (), s32[]{:S(2)}) async-start(), calls=%async_computation.1 | async-start | bytes 1114112 | tf_op jit(solution)/shard_map/all_gather | solution.py:47
  424.2 43.3 %copy-start.3 = (f32[1024]{0:T(1024)}, f32[1024]{0:T(1024)S(1)}, u32[]{:S(2)}) copy-start(f32[1024]{0:T(1024)S(1)} %add_multiply_fusion.1) | copy-start | bytes 12292
Sparse Core Ops, SparseCore 0:
  13.7 49.8 all-gather.5
  65.4 39.5 all-gather.7
